TPU v7x, 32 devices: a whole 2x2x4 slice. The times are simulated.
32 devices in a mesh: row: 4 (over y, x), col: 8 (over z, core).
Axes of the slice: x: 2, y: 2, z: 4, core: 2. Of those that a mesh axis runs over, the one named last changes fastest.
Arguments:
- features: bfloat16 [8192, 512], P(('col', 'row')), may hold values from -6 to 6
- order: int32 [8192], P('col'), may hold values from 0 to 8191, as said below
- tile_count: int32 [4, 8], P('row', 'col'), may hold values from 1 to 16, as said below
- tile_slots: int32 [4, 8, 16], P('row', 'col'), may hold values from 0 to 127, as said below
- blocks: bfloat16 [4, 8, 16, 128, 128], P('row', 'col'), may hold values from -0.3125 to 0.3125
- weight: bfloat16 [512, 512], replicated, may hold values from -0.25 to 0.25
Outputs:
- updated: bfloat16 [8192, 512], P(('row', 'col'))
Inputs may be any that keep to these rules, and one draw needn't show every extreme that they name: order permutes each column group: positions j * 8 * 128 to (j + 1) * 8 * 128 - 1 name each node of that same range once. `tile_count`: some tile lists exactly 16 blocks in every draw. `tile_slots`: the codes of one tile's slots are distinct; slots at or beyond its count are unused.
All inputs are finite; a program needn't handle non-finite values.
Results may differ from a plain program's by a relative error of at most 0.01.
Values may be sent and summed in bfloat16 or wider, within the bound.
No kernel may reach another device: no remote copies, remote signals or barrier semaphores. Data moves between devices by JAX's collectives and lax.ppermute only.
A program may use at most 64 MiB of HBM per device.

v0:
```python
import jax
import jax.numpy as jnp
from jax import lax
from jax.sharding import PartitionSpec as P


def add_slots(partial_value, tile_blocks, codes, column_x, first, last, offset, colblk, width):

    def step(slot, total):
        code = codes[slot]
        block_row = code // colblk
        block_col = code % colblk
        xblock = lax.dynamic_slice_in_dim(column_x, block_col * width, width, 0)
        product = jnp.dot(tile_blocks[slot - offset], xblock, preferred_element_type=jnp.float32)
        rows = lax.dynamic_slice_in_dim(total, block_row * width, width, 0)
        return lax.dynamic_update_slice_in_dim(total, rows + product, block_row * width, 0)

    return lax.fori_loop(first, last, step, partial_value)


def per_device(features, order, tile_count, tile_slots, blocks, weight):
    corpus = lax.all_gather(features, "row", axis=0, tiled=True)
    group = corpus.shape[0]
    width = blocks.shape[-1]
    feats = weight.shape[0]
    colblk = group // width
    rowblk = colblk * lax.axis_size("col") // lax.axis_size("row")
    local_index = order - lax.axis_index("col") * group
    column_x = jnp.take(corpus, local_index, axis=0)
    count = tile_count[0, 0]
    codes = tile_slots[0, 0]
    tile_blocks = blocks[0, 0]
    empty = jnp.zeros((rowblk * width, feats), jnp.float32)
    partial_value = add_slots(empty, tile_blocks, codes, column_x, 0, count, 0, colblk, width)
    summed = lax.psum_scatter(
        partial_value.astype(jnp.bfloat16), "col", scatter_dimension=0, tiled=True
    )
    projected = jnp.dot(summed, weight, preferred_element_type=jnp.float32)
    return jax.nn.relu(projected).astype(jnp.bfloat16)


def solution(mesh):
    in_specs = (
        P(("col", "row"), None),
        P("col"),
        P("row", "col"),
        P("row", "col", None),
        P("row", "col", None, None, None),
        P(),
    )
    out_specs = P(("row", "col"), None)
    return jax.shard_map(
        per_device, mesh=mesh, in_specs=in_specs, out_specs=out_specs, check_vma=False
    )
```

profile of v0, /device:TPU:0, one launch (start us, length us, event | category | flops | bytes accessed | tf_op | source)
XLA Modules:
  0.0 184.2 jit_solution(3299845912128744805)
XLA Ops:
  6.5 0.7 all-gather.2.cloned.1.call-update
  7.3 0.7 compare_and_fusion
  8.0 0.7 fusion.6
  8.7 29.9 %all-gather.2.cloned.1.call-done = bf16[1024,512]{1,0:T(8,128)(2,1)} async-done(((bf16[256,512]{1,0:T(8,128)(2,1)}), bf16[1024,512]{1,0:T(8,128)(2,1)}) %all-gather.2.cloned.1.call-update) | async-done | bytes 1048592 | tf_op jit(solution)/shard_map/all_gather | solution.py:22
  38.6 5.3 %gather_fusion = bf16[1024,512]{1,0:T(8,128)(2,1)S(1)} fusion(bf16[1024,512]{1,0:T(8,128)(2,1)} %all-gather.2.cloned.1.call-done, s32[1024]{0:T(1024)S(1)} %fusion.6), kind=kCustom, calls=%fused_computation | custom fusion | bytes 2101248 | tf_op jit(solution)/shard_map/jit(_take)/gather | solution.py:29
  44.1 2.5 %broadcast_in_dim.15 = f32[2048,512]{1,0:T(8,128)} broadcast(f32[]{:T(128)} %constant.88.clone.1), dimensions={} | broadcast | bytes 4194308 | tf_op jit(solution)/shard_map/broadcast_in_dim | solution.py:33
  46.6 45.5 %while.12 = (s32[]{:T(128)}, f32[2048,512]{1,0:T(8,128)}, s32[]{:T(128)}, s32[16]{0:T(128)S(1)}, bf16[16,128,128]{2,1,0:T(8,128)(2,1)}, /*index=5*/bf16[1024,512...) while((s32[]{:T(128)}, f32[2048,512]{1,0:T(8,128)}, ...), condition=%wide.region_1.2_spmd, body=%wide.region_0.1_spmd.sunk | while | flops 16842784 | bytes 688622 | solution.py:18
  47.3 0.6 dynamic_slice.38
  50.4 1.9 %fusion.14 = f32[2048,512]{1,0:T(8,128)} fusion(f32[2048,512]{1,0:T(8,128)} %get-tuple-element.156, s32[]{:T(128)S(6)} %select_n.63, bf16[1024,512]{1,0:T(8,128)(2,1)S(1)} %get-tuple-element.176, s32[]{:T(128)S(6)} %select_n.65, bf16[16,128,128]{2,1,0:T(8,128)(2,1)} %get-tuple-element.175, s32[]{:T(128)S(6)} %select_n.61), kind=kOutput, calls=%fused_computation.2.clone.1 | convolution fusion | flops 16842752 | bytes 688140 | tf_op jit(solution)/shard_map/while/body/dot_general | solution.py:14
  52.9 0.6 dynamic_slice.38
  56.0 1.9 %fusion.14 = f32[2048,512]{1,0:T(8,128)} fusion(f32[2048,512]{1,0:T(8,128)} %get-tuple-element.156, s32[]{:T(128)S(6)} %select_n.63, bf16[1024,512]{1,0:T(8,128)(2,1)S(1)} %get-tuple-element.176, s32[]{:T(128)S(6)} %select_n.65, bf16[16,128,128]{2,1,0:T(8,128)(2,1)} %get-tuple-element.175, s32[]{:T(128)S(6)} %select_n.61), kind=kOutput, calls=%fused_computation.2.clone.1 | convolution fusion | flops 16842752 | bytes 688140 | tf_op jit(solution)/shard_map/while/body/dot_general | solution.py:14
  61.6 1.9 %fusion.14 = f32[2048,512]{1,0:T(8,128)} fusion(f32[2048,512]{1,0:T(8,128)} %get-tuple-element.156, s32[]{:T(128)S(6)} %select_n.63, bf16[1024,512]{1,0:T(8,128)(2,1)S(1)} %get-tuple-element.176, s32[]{:T(128)S(6)} %select_n.65, bf16[16,128,128]{2,1,0:T(8,128)(2,1)} %get-tuple-element.175, s32[]{:T(128)S(6)} %select_n.61), kind=kOutput, calls=%fused_computation.2.clone.1 | convolution fusion | flops 16842752 | bytes 688140 | tf_op jit(solution)/shard_map/while/body/dot_general | solution.py:14
  67.2 1.9 %fusion.14 = f32[2048,512]{1,0:T(8,128)} fusion(f32[2048,512]{1,0:T(8,128)} %get-tuple-element.156, s32[]{:T(128)S(6)} %select_n.63, bf16[1024,512]{1,0:T(8,128)(2,1)S(1)} %get-tuple-element.176, s32[]{:T(128)S(6)} %select_n.65, bf16[16,128,128]{2,1,0:T(8,128)(2,1)} %get-tuple-element.175, s32[]{:T(128)S(6)} %select_n.61), kind=kOutput, calls=%fused_computation.2.clone.1 | convolution fusion | flops 16842752 | bytes 688140 | tf_op jit(solution)/shard_map/while/body/dot_general | solution.py:14
  69.7 0.6 dynamic_slice.38
  72.8 1.9 %fusion.14 = f32[2048,512]{1,0:T(8,128)} fusion(f32[2048,512]{1,0:T(8,128)} %get-tuple-element.156, s32[]{:T(128)S(6)} %select_n.63, bf16[1024,512]{1,0:T(8,128)(2,1)S(1)} %get-tuple-element.176, s32[]{:T(128)S(6)} %select_n.65, bf16[16,128,128]{2,1,0:T(8,128)(2,1)} %get-tuple-element.175, s32[]{:T(128)S(6)} %select_n.61), kind=kOutput, calls=%fused_computation.2.clone.1 | convolution fusion | flops 16842752 | bytes 688140 | tf_op jit(solution)/shard_map/while/body/dot_general | solution.py:14
  75.3 0.6 dynamic_slice.38
  78.4 1.9 %fusion.14 = f32[2048,512]{1,0:T(8,128)} fusion(f32[2048,512]{1,0:T(8,128)} %get-tuple-element.156, s32[]{:T(128)S(6)} %select_n.63, bf16[1024,512]{1,0:T(8,128)(2,1)S(1)} %get-tuple-element.176, s32[]{:T(128)S(6)} %select_n.65, bf16[16,128,128]{2,1,0:T(8,128)(2,1)} %get-tuple-element.175, s32[]{:T(128)S(6)} %select_n.61), kind=kOutput, calls=%fused_computation.2.clone.1 | convolution fusion | flops 16842752 | bytes 688140 | tf_op jit(solution)/shard_map/while/body/dot_general | solution.py:14
  81.0 0.6 dynamic_slice.38
  84.0 1.9 %fusion.14 = f32[2048,512]{1,0:T(8,128)} fusion(f32[2048,512]{1,0:T(8,128)} %get-tuple-element.156, s32[]{:T(128)S(6)} %select_n.63, bf16[1024,512]{1,0:T(8,128)(2,1)S(1)} %get-tuple-element.176, s32[]{:T(128)S(6)} %select_n.65, bf16[16,128,128]{2,1,0:T(8,128)(2,1)} %get-tuple-element.175, s32[]{:T(128)S(6)} %select_n.61), kind=kOutput, calls=%fused_computation.2.clone.1 | convolution fusion | flops 16842752 | bytes 688140 | tf_op jit(solution)/shard_map/while/body/dot_general | solution.py:14
  86.6 0.6 dynamic_slice.38
  89.7 1.8 %fusion.14 = f32[2048,512]{1,0:T(8,128)} fusion(f32[2048,512]{1,0:T(8,128)} %get-tuple-element.156, s32[]{:T(128)S(6)} %select_n.63, bf16[1024,512]{1,0:T(8,128)(2,1)S(1)} %get-tuple-element.176, s32[]{:T(128)S(6)} %select_n.65, bf16[16,128,128]{2,1,0:T(8,128)(2,1)} %get-tuple-element.175, s32[]{:T(128)S(6)} %select_n.61), kind=kOutput, calls=%fused_computation.2.clone.1 | convolution fusion | flops 16842752 | bytes 688140 | tf_op jit(solution)/shard_map/while/body/dot_general | solution.py:14
  92.2 3.8 %convert_element_type.6 = bf16[2048,512]{1,0:T(8,128)(2,1)} convert(f32[2048,512]{1,0:T(8,128)} %get-tuple-element.88) | non-fusion elementwise | flops 1048576 | bytes 6291456 | tf_op jit(solution)/shard_map/convert_element_type | solution.py:36
  95.9 79.4 %reduce-scatter.2.cloned.1.call-done = bf16[256,512]{1,0:T(8,128)(2,1)} async-done(((bf16[2048,512]{1,0:T(8,128)(2,1)}), bf16[256,512]{1,0:T(8,128)(2,1)}) %reduce-scatter.2.cloned.1.call-update) | async-done | bytes 262160 | tf_op jit(solution)/shard_map/reduce_scatter | solution.py:35
  175.4 2.0 %fusion.5 = bf16[256,512]{1,0:T(8,128)(2,1)} fusion(bf16[256,512]{1,0:T(8,128)(2,1)} %reduce-scatter.2.cloned.1.call-done, bf16[512,512]{1,0:T(8,128)(2,1)S(1)} %copy-done), kind=kOutput, calls=%fused_computation.8 | convolution fusion | flops 134479872 | bytes 1048576 | tf_op jit(solution)/shard_map/dot_general | solution.py:38
  (10 shorter events, 1.5 us)
Async XLA Ops:
  6.5 168.8 %copy-start = (bf16[512,512]{1,0:T(8,128)(2,1)S(1)}, bf16[512,512]{1,0:T(8,128)(2,1)}, u32[]{:S(2)}) copy-start(bf16[512,512]{1,0:T(8,128)(2,1)} %param.13) | copy-start | bytes 1572868
  6.5 32.0 %all-gather.2.cloned.1.call-start = ((), (), s32[]{:S(2)}) async-start(), calls=%async_computation.1 | async-start | bytes 1310720 | tf_op jit(solution)/shard_map/all_gather | solution.py:22
  7.3 168.1 %reduce-scatter.2.cloned.1.call-start = ((), (), s32[]{:S(2)}) async-start(), calls=%async_computation.2 | async-start | bytes 2359296 | tf_op jit(solution)/shard_map/reduce_scatter | solution.py:35
  43.9 2.7 %copy-start.1 = (s32[1,1,16]{2,1,0:T(1,128)S(1)}, s32[1,1,16]{2,1,0:T(1,128)}, u32[]{:S(2)}) copy-start(s32[1,1,16]{2,1,0:T(1,128)} %param.11) | copy-start | bytes 196
Sparse Core Ops, SparseCore 0:
  9.2 29.3 all-gather.1
  96.1 79.2 reduce-scatter.1
where the time goes:
time: 185 us; the launch traced here: 184 us
  waiting for transfers between devices  110 us (59%)
  loops' own time  25.9 us (14%)
  matrix products  16.8 us (9%)
  between operations  13.4 us (7%)
  local copies, waits for them, and re-layouts  12.6 us (7%)
  other arithmetic  5.36 us (3%)
    reduce_scatter x1, waiting for transfers between devices, per_device(): lax.psum_scatter(partial_value.astype(jnp.bfloat16), 'col', scatter_dimen...  79.4 us
    all_gather x1, waiting for transfers between devices, per_device(): corpus = lax.all_gather(features, 'row', axis=0, tiled=True)  29.9 us
    another operation x1, loops' own time, add_slots(): return lax.fori_loop(first, last, step, partial_value)  25.9 us
    dot_general x8, matrix products, step(): jnp.dot(tile_blocks[slot - offset], xblock, preferred_element_type=jnp.fl...  14.8 us
    gather x1, local copies, waits for them, and re-layouts, per_device(): column_x = jnp.take(corpus, local_index, axis=0)  5.35 us
    dynamic_slice x8, local copies, waits for them, and re-layouts, step(): code = codes[slot]  4.74 us
    convert_element_type x1, other arithmetic, per_device(): partial_value.astype(jnp.bfloat16)  3.77 us
  transfers between devices with their start and end apart: 2, of which 2 were waited for; matrix products, arithmetic and copies ran while one was open for 1% of the time, Pallas kernels for 0%

commit v1 on v0

v1 whole, which is shorter than its diff:
```python
import functools

import jax
import jax.numpy as jnp
from jax import lax
from jax.experimental import pallas as pl
from jax.experimental.pallas import tpu as pltpu
from jax.sharding import PartitionSpec as P

VMEM_LIMIT = 48 * 1024 * 1024
PARTS = 1


def chunk_slot(dest, here, chips):
    if chips != 4:
        return lax.rem(dest - here + chips, chips)
    even = lax.rem(here, 2) == 0
    first = jnp.where(even, 3, 0)
    second = lax.rem(here + 2, 4)
    return jnp.where(dest == here, 0, jnp.where(dest == second, 2, jnp.where(dest == first, 1, 3)))


def tile_kernel(chips, rows, shard, order_ref, count_ref, slots_ref, blocks_ref, keep_ref, give_ref):
    group = keep_ref.shape[1]
    width = blocks_ref.shape[-1]
    colblk = group // width
    piece = min(rows, width)
    me = lax.axis_index("col")
    row = lax.axis_index("row")
    chip, core = me // 2, lax.rem(me, 2)
    keep_ref[...] = jnp.zeros_like(keep_ref)
    give_ref[...] = jnp.zeros_like(give_ref)
    place = lax.broadcasted_iota(jnp.int32, (group, width), 0)
    corpus = ((place // shard) ^ row) * shard + place % shard + me * group

    def step(slot, carry):
        code = slots_ref[0, 0, slot]
        block_row = code // colblk
        block_col = lax.rem(code, colblk)
        nodes = order_ref[pl.ds(block_col, 1), :]
        onehot = jnp.where(corpus == nodes, 1.0, 0.0).astype(jnp.bfloat16)
        moved = lax.dot_general(
            blocks_ref[0, 0, slot], onehot, (((1,), (1,)), ((), ())),
            preferred_element_type=jnp.float32,
        ).astype(jnp.bfloat16)
        for part in range(width // piece):
            start = block_row * width + part * piece
            dest = start // rows
            at = chunk_slot(dest // 2, chip, chips) * rows + lax.rem(start, rows)
            at = pl.multiple_of(at, piece)
            values = moved[part * piece:(part + 1) * piece]

            @pl.when(lax.rem(dest, 2) == core)
            def _():
                keep_ref[pl.ds(at, piece), :] += values

            @pl.when(lax.rem(dest, 2) != core)
            def _():
                give_ref[pl.ds(at, piece), :] += values

        return carry

    lax.fori_loop(0, count_ref[0, 0], step, 0)


def sum_kernel(shards, own_tile_ref, other_tile_ref, *refs):
    features, outs = refs[:2 * shards], refs[2 * shards:]
    x = jnp.concatenate([ref[...] for ref in features[:shards]], axis=0)
    y = jnp.concatenate([ref[...] for ref in features[shards:]], axis=0)
    rows = outs[0].shape[0]
    for k, out in enumerate(outs):
        here = slice(k * rows, (k + 1) * rows)
        total = jnp.dot(own_tile_ref[here, :], x, preferred_element_type=jnp.float32)
        total += jnp.dot(other_tile_ref[here, :], y, preferred_element_type=jnp.float32)
        out[...] = total.astype(out.dtype)


def project_kernel(terms, *refs):
    ends_ref, weight_ref, out_ref = refs[-3], refs[-2], refs[-1]
    depth = refs[0].shape[1]
    projected = None
    for part in range((len(refs) - 3) // terms):
        mine = refs[part * terms:(part + 1) * terms]
        total = mine[0][...]
        for ref in mine[2:]:
            total += ref[...].astype(jnp.float32)
        first = mine[1][...].astype(jnp.float32)
        total += jnp.where(ends_ref[0] == 1, first, jnp.zeros_like(first))
        product = jnp.dot(
            total.astype(jnp.bfloat16), weight_ref[part * depth:(part + 1) * depth, :],
            preferred_element_type=jnp.float32,
        )
        projected = product if projected is None else projected + product
    out_ref[...] = jnp.maximum(projected, 0.0).astype(out_ref.dtype)


def over_chips(x, pairs):
    return lax.ppermute(x, "col", [(2 * a + c, 2 * b + c) for a, b in pairs for c in range(2)])


def per_device(features, order, tile_count, tile_slots, blocks, weight):
    rows_axis, cols_axis = lax.axis_size("row"), lax.axis_size("col")
    chips = cols_axis // 2
    shard, feats = features.shape
    group = shard * rows_axis
    width = blocks.shape[-1]
    rows = group // rows_axis
    params = pltpu.CompilerParams(vmem_limit_bytes=VMEM_LIMIT)
    smem = pl.BlockSpec(memory_space=pltpu.SMEM)
    vmem = pl.BlockSpec(memory_space=pltpu.VMEM)
    bf16 = jnp.bfloat16

    def other_core(x):
        return lax.ppermute(x, "col", [(j, j ^ 1) for j in range(cols_axis)])

    keep, give = pl.pallas_call(
        functools.partial(tile_kernel, chips, rows, shard),
        out_shape=[jax.ShapeDtypeStruct((chips * rows, group), bf16)] * 2,
        in_specs=[vmem, smem, smem, vmem],
        out_specs=[vmem, vmem],
        compiler_params=params,
    )(order.reshape(group // width, width), tile_count, tile_slots, blocks)
    other = other_core(give)

    depth = feats // PARTS
    chip = lax.axis_index("col") // 2
    ends = ((chip == 0) | (chip == chips - 1)) if chips == 4 else (chip >= 0)
    parts = []
    for part in range(PARTS):
        mine = features if PARTS == 1 else features[:, part * depth:(part + 1) * depth]
        gathered = [mine]
        for k in range(1, rows_axis):
            gathered.append(lax.ppermute(mine, "row", [(i, i ^ k) for i in range(rows_axis)]))
        swapped = [other_core(x) for x in gathered]
        sums = pl.pallas_call(
            functools.partial(sum_kernel, rows_axis),
            out_shape=[jax.ShapeDtypeStruct((rows, depth), jnp.float32)]
            + [jax.ShapeDtypeStruct((rows, depth), bf16)] * (chips - 1),
            in_specs=[vmem] * (2 + 2 * rows_axis),
            out_specs=[vmem] * chips,
            compiler_params=params,
        )(keep, other, *gathered, *swapped)
        if chips == 4:
            own, far, across, near = sums
            first = over_chips(far, [(0, 1), (1, 0), (2, 3), (3, 2)])
            inner = over_chips(near, [(1, 2), (2, 1)])
            added = jnp.where(ends, across, (across.astype(jnp.float32) + first.astype(jnp.float32)).astype(bf16))
            near, added = lax.optimization_barrier((near, added))
            outer = over_chips(near, [(0, 1), (3, 2)])
            last = over_chips(added, [(0, 2), (2, 0), (1, 3), (3, 1)])
            parts.append([own, first, inner, outer, last])
        else:
            received = [
                over_chips(sums[k], [(a, (a + k) % chips) for a in range(chips)])
                for k in range(1, chips)
            ]
            parts.append([sums[0], *received])
    terms = len(parts[0])
    return pl.pallas_call(
        functools.partial(project_kernel, terms),
        out_shape=jax.ShapeDtypeStruct((rows, feats), bf16),
        in_specs=[vmem] * (terms * PARTS) + [smem, vmem],
        out_specs=vmem,
        compiler_params=params,
    )(*[x for part in parts for x in part], ends.astype(jnp.int32).reshape(1), weight)


def solution(mesh):
    in_specs = (
        P(("col", "row"), None),
        P("col"),
        P("row", "col"),
        P("row", "col", None),
        P("row", "col", None, None, None),
        P(),
    )
    out_specs = P(("row", "col"), None)
    return jax.shard_map(
        per_device, mesh=mesh, in_specs=in_specs, out_specs=out_specs, check_vma=False
    )
```

time: 185 us -> 59 us (0.32)
  waiting for transfers between devices: 110 us -> 34 us
  loops' own time: 25.9 us -> 0 us
  matrix products: 16.8 us -> 0 us
  starting transfers between devices: 0.04 us -> 13.5 us
  between operations: 13.4 us -> 0.72 us
  local copies, waits for them, and re-layouts: 12.6 us -> 4.67 us
  Pallas kernels: 0 us -> 6.23 us
  other arithmetic: 5.36 us -> 0.08 us
    reduce_scatter x1 -> x0, waiting for transfers between devices: 79.4 us -> none  [per_device(): lax.psum_scatter(partial_value.astype(jnp.bfloat16), 'col', scatter_dimen...]
    ppermute x0 -> x12, waiting for transfers between devices: none -> 34 us  [the longest x4 20.1 us: over_chips(): lax.ppermute(x, 'col', [(2 * a + c, 2 * b + c) for a, b in pairs for c in...]
    all_gather x1 -> x0, waiting for transfers between devices: 29.9 us -> none  [per_device(): corpus = lax.all_gather(features, 'row', axis=0, tiled=True)]
    another operation x1 -> x0, loops' own time: 25.9 us -> none  [add_slots(): return lax.fori_loop(first, last, step, partial_value)]
    dot_general x9 -> x0, matrix products: 16.8 us -> none  [the longest x8 14.8 us: step(): jnp.dot(tile_blocks[slot - offset], xblock, preferred_element_type=jnp.fl...]
    ppermute x0 -> x12, starting transfers between devices: none -> 13.5 us  [the longest x3 6.51 us: per_device(): lax.ppermute(mine, 'row', [(i, i ^ k) for i in range(rows_axis)])]
    pallas_call x0 -> x3, Pallas kernels: none -> 6.23 us  [the longest x1 3.97 us: per_device(): pl.pallas_call(functools.partial(sum_kernel, rows_axis), out_shape=[jax.S...]
    gather x1 -> x0, local copies, waits for them, and re-layouts: 5.35 us -> none  [per_device(): column_x = jnp.take(corpus, local_index, axis=0)]
  transfers between devices with their start and end apart: 2 -> 12, of which waited for: 2 -> 7; matrix products, arithmetic and copies ran while one was open for 1% -> 0% of each run, Pallas kernels for 0% -> 0%
where the time goes in v1:
time: 59 us; the launch traced here: 59.3 us
  waiting for transfers between devices  34 us (58%)
  starting transfers between devices  13.5 us (23%)
  Pallas kernels  6.23 us (11%)
  local copies, waits for them, and re-layouts  4.67 us (8%)
  between operations  0.72 us (1%)
    ppermute x4, waiting for transfers between devices, over_chips(): lax.ppermute(x, 'col', [(2 * a + c, 2 * b + c) for a, b in pairs for c in...  20.1 us
    ppermute x3, waiting for transfers between devices, per_device(): lax.ppermute(mine, 'row', [(i, i ^ k) for i in range(rows_axis)])  12.4 us
    ppermute x3, starting transfers between devices, per_device(): lax.ppermute(mine, 'row', [(i, i ^ k) for i in range(rows_axis)])  6.51 us
    ppermute x4, starting transfers between devices, over_chips(): lax.ppermute(x, 'col', [(2 * a + c, 2 * b + c) for a, b in pairs for c in...  5.13 us
    unnamed x12, local copies, waits for them, and re-layouts  4.67 us
    pallas_call x1, Pallas kernels, per_device(): pl.pallas_call(functools.partial(sum_kernel, rows_axis), out_shape=[jax.S...  3.97 us
    ppermute x5, starting transfers between devices, other_core(): return lax.ppermute(x, 'col', [(j, j ^ 1) for j in range(cols_axis)])  1.89 us
    ppermute x5, waiting for transfers between devices, other_core(): return lax.ppermute(x, 'col', [(j, j ^ 1) for j in range(cols_axis)])  1.52 us
  transfers between devices with their start and end apart: 12, of which 7 were waited for; matrix products, arithmetic and copies ran while one was open for 0% of the time, Pallas kernels for 0%

profile of v1, /device:TPU:0, one launch (start us, length us, event | category | flops | bytes accessed | tf_op | source)
XLA Modules:
  0.0 59.3 jit_solution(4535994026240006395)
XLA Ops:
  0.7 1.0 %copy-done.1 = bf16[1,1,16,128,128]{4,3,2,1,0:T(8,128)(2,1)S(1)} copy-done((bf16[1,1,16,128,128]{4,3,2,1,0:T(8,128)(2,1)S(1)}, bf16[1,1,16,128,128]{4,3,2,1,0:T(8,128)(2,1)}, u32[]{:S(2)}) %copy-start.1) | copy-done | bytes 524312
  1.7 0.7 %copy-done.3 = s32[1024]{0:T(1024)S(1)} copy-done((s32[1024]{0:T(1024)S(1)}, s32[1024]{0:T(1024)}, u32[]{:S(2)}) %copy-start.3) | copy-done | bytes 4120
  2.4 0.7 %copy-done.4 = s32[1,1,16]{2,1,0:T(1,128)S(1)} copy-done((s32[1,1,16]{2,1,0:T(1,128)S(1)}, s32[1,1,16]{2,1,0:T(1,128)}, u32[]{:S(2)}) %copy-start.4) | copy-done | bytes 88
  3.0 1.2 %shard_map.64 = (bf16[1024,1024]{1,0:T(8,128)(2,1)S(1)}, bf16[1024,1024]{1,0:T(8,128)(2,1)S(1)}) custom-call(s32[8,128]{1,0:T(8,128)S(1)} %bitcast.2, s32[1,1]{1,0:T(1,128)S(6)} %copy.7.count_ref, s32[1,1,16]{2,1,0:T(1,128)S(1)} %copy-done.4, bf16[1,1,16,128,128]{4,3,2,1,0:T(8,128)(2,1)S(1)} %copy-done.1), custom_call_target="tpu_custom_call" | custom-call | tf_op jit(solution)/shard_map/pallas_call | solution.py:116
  4.3 1.9 %collective-permute-start = (bf16[1024,1024]{1,0:T(8,128)(2,1)S(1)}, bf16[1024,1024]{1,0:T(8,128)(2,1)S(1)}, u32[]{:S(2)}, u32[]{:S(2)}) collective-permute-start(bf16[1024,1024]{1,0:T(8,128)(2,1)S(1)} %get-tuple-element.14), channel_id=1, source_target_pairs={{0,1},{1,0},{2,3},{3,2},{4,5},{5,4},{6,7},{7,6},{8,9},{9,8},{10,11... | collective-permute-start | bytes 6291464 | tf_op jit(solution)/shard_map/ppermute | solution.py:114
  6.2 3.4 %collective-permute-start.1 = (bf16[256,512]{1,0:T(8,128)(2,1)}, bf16[256,512]{1,0:T(8,128)(2,1)S(1)}, u32[]{:S(2)}, u32[]{:S(2)}) collective-permute-start(bf16[256,512]{1,0:T(8,128)(2,1)} %refs_0_.1), channel_id=1, source_target_pairs={{0,8},{8,0},{16,24},{24,16},{1,9},{9,1},{17,25},{25,17},{2,10},{10... | collective-permute-start | bytes 786440 | tf_op jit(solution)/shard_map/ppermute | solution.py:133
  9.6 1.7 %collective-permute-start.2 = (bf16[256,512]{1,0:T(8,128)(2,1)}, bf16[256,512]{1,0:T(8,128)(2,1)S(1)}, u32[]{:S(2)}, u32[]{:S(2)}) collective-permute-start(bf16[256,512]{1,0:T(8,128)(2,1)} %refs_0_.1), channel_id=1, source_target_pairs={{0,16},{8,24},{16,0},{24,8},{1,17},{9,25},{17,1},{25,9},{2,18},{10... | collective-permute-start | bytes 786440 | tf_op jit(solution)/shard_map/ppermute | solution.py:133
  11.3 1.4 %collective-permute-start.3 = (bf16[256,512]{1,0:T(8,128)(2,1)}, bf16[256,512]{1,0:T(8,128)(2,1)S(1)}, u32[]{:S(2)}, u32[]{:S(2)}) collective-permute-start(bf16[256,512]{1,0:T(8,128)(2,1)} %refs_0_.1), channel_id=1, source_target_pairs={{0,24},{8,16},{16,8},{24,0},{1,25},{9,17},{17,9},{25,1},{2,26},{10... | collective-permute-start | bytes 786440 | tf_op jit(solution)/shard_map/ppermute | solution.py:133
  12.7 4.2 %collective-permute-done.1.refs_1_ = bf16[256,512]{1,0:T(8,128)(2,1)S(1)} collective-permute-done((bf16[256,512]{1,0:T(8,128)(2,1)}, bf16[256,512]{1,0:T(8,128)(2,1)S(1)}, u32[]{:S(2)}, u32[]{:S(2)}) %collective-permute-start.1) | collective-permute-done | bytes 262176 | tf_op jit(solution)/shard_map/ppermute | solution.py:133
  16.9 6.4 %collective-permute-done.2.refs_2_ = bf16[256,512]{1,0:T(8,128)(2,1)S(1)} collective-permute-done((bf16[256,512]{1,0:T(8,128)(2,1)}, bf16[256,512]{1,0:T(8,128)(2,1)S(1)}, u32[]{:S(2)}, u32[]{:S(2)}) %collective-permute-start.2) | collective-permute-done | bytes 262176 | tf_op jit(solution)/shard_map/ppermute | solution.py:133
  23.3 1.8 %collective-permute-done.3.refs_3_ = bf16[256,512]{1,0:T(8,128)(2,1)S(1)} collective-permute-done((bf16[256,512]{1,0:T(8,128)(2,1)}, bf16[256,512]{1,0:T(8,128)(2,1)S(1)}, u32[]{:S(2)}, u32[]{:S(2)}) %collective-permute-start.3) | collective-permute-done | bytes 262176 | tf_op jit(solution)/shard_map/ppermute | solution.py:133
  25.2 1.5 %collective-permute-done.7.refs_7_ = bf16[256,512]{1,0:T(8,128)(2,1)S(1)} collective-permute-done((bf16[256,512]{1,0:T(8,128)(2,1)S(1)}, bf16[256,512]{1,0:T(8,128)(2,1)S(1)}, u32[]{:S(2)}, u32[]{:S(2)}) %collective-permute-start.7) | collective-permute-done | bytes 262176 | tf_op jit(solution)/shard_map/ppermute | solution.py:114
  26.7 1.3 %copy-done.5 = bf16[1024,1024]{1,0:T(8,128)(2,1)} copy-done((bf16[1024,1024]{1,0:T(8,128)(2,1)}, bf16[1024,1024]{1,0:T(8,128)(2,1)S(1)}, u32[]{:S(2)}) %copy-start.5) | copy-done | bytes 2097176
  28.0 0.9 %copy-done.2 = bf16[256,512]{1,0:T(8,128)(2,1)S(1)} copy-done((bf16[256,512]{1,0:T(8,128)(2,1)S(1)}, bf16[256,512]{1,0:T(8,128)(2,1)}, u32[]{:S(2)}) %copy-start.2) | copy-done | bytes 262168
  29.0 4.0 %shard_map.65 = (f32[256,512]{1,0:T(8,128)S(1)}, bf16[256,512]{1,0:T(8,128)(2,1)S(1)}, bf16[256,512]{1,0:T(8,128)(2,1)S(1)}, bf16[256,512]{1,0:T(8,128)(2,1)S(1)}) custom-call(bf16[1024,1024]{1,0:T(8,128)(2,1)S(1)} %get-tuple-element.13.own_tile_ref, bf16[1024,1024]{1,0:T(8,128)(2,1)} %copy-done.5, bf16[256,512]{1,0:T(8,128)(2,1)S(1)} %copy-done.2, ...), custom_call_target="tpu_custom_call" | custom-call | tf_op jit(solution)/shard_map/pallas_call | solution.py:135
  32.9 1.1 %collective-permute-start.8 = (bf16[256,512]{1,0:T(8,128)(2,1)S(1)}, bf16[256,512]{1,0:T(8,128)(2,1)S(1)}, u32[]{:S(2)}, u32[]{:S(2)}) collective-permute-start(bf16[256,512]{1,0:T(8,128)(2,1)S(1)} %get-tuple-element.16), channel_id=1, source_target_pairs={{0,2},{1,3},{2,0},{3,1},{4,6},{5,7},{6,4},{7,5},{8,10},{9,11},{10,... | collective-permute-start | bytes 786440 | tf_op jit(solution)/shard_map/ppermute | solution.py:98
  34.1 0.7 %collective-permute-start.9 = (bf16[256,512]{1,0:T(8,128)(2,1)S(1)}, bf16[256,512]{1,0:T(8,128)(2,1)S(1)}, u32[]{:S(2)}, u32[]{:S(2)}) collective-permute-start(bf16[256,512]{1,0:T(8,128)(2,1)S(1)} %get-tuple-element.19), channel_id=1, source_target_pairs={{2,4},{3,5},{4,2},{5,3},{10,12},{11,13},{12,10},{13,11},{18,20},{1... | collective-permute-start | bytes 786440 | tf_op jit(solution)/shard_map/ppermute | solution.py:98
  34.7 6.6 %collective-permute-done.8.refs_1_ = bf16[256,512]{1,0:T(8,128)(2,1)S(1)} collective-permute-done((bf16[256,512]{1,0:T(8,128)(2,1)S(1)}, bf16[256,512]{1,0:T(8,128)(2,1)S(1)}, u32[]{:S(2)}, u32[]{:S(2)}) %collective-permute-start.8) | collective-permute-done | bytes 262176 | tf_op jit(solution)/shard_map/ppermute | solution.py:98
  41.4 0.1 fusion
  41.4 3.0 %collective-permute-start.10 = (bf16[256,512]{1,0:T(8,128)(2,1)S(1)}, bf16[256,512]{1,0:T(8,128)(2,1)S(1)}, u32[]{:S(2)}, u32[]{:S(2)}) collective-permute-start(bf16[256,512]{1,0:T(8,128)(2,1)S(1)} %get-tuple-element.19), channel_id=1, source_target_pairs={{0,2},{1,3},{6,4},{7,5},{8,10},{9,11},{14,12},{15,13},{16,18},{17,... | collective-permute-start | bytes 786440 | tf_op jit(solution)/shard_map/ppermute | solution.py:98
  44.4 0.4 collective-permute-start.11
  44.8 6.3 %collective-permute-done.10.refs_3_ = bf16[256,512]{1,0:T(8,128)(2,1)S(1)} collective-permute-done((bf16[256,512]{1,0:T(8,128)(2,1)S(1)}, bf16[256,512]{1,0:T(8,128)(2,1)S(1)}, u32[]{:S(2)}, u32[]{:S(2)}) %collective-permute-start.10) | collective-permute-done | bytes 262176 | tf_op jit(solution)/shard_map/ppermute | solution.py:98
  51.1 7.1 %collective-permute-done.11.refs_4_ = bf16[256,512]{1,0:T(8,128)(2,1)S(1)} collective-permute-done((bf16[256,512]{1,0:T(8,128)(2,1)S(1)}, bf16[256,512]{1,0:T(8,128)(2,1)S(1)}, u32[]{:S(2)}, u32[]{:S(2)}) %collective-permute-start.11) | collective-permute-done | bytes 262176 | tf_op jit(solution)/shard_map/ppermute | solution.py:98
  58.2 1.0 %shard_map.66 = bf16[256,512]{1,0:T(8,128)(2,1)} custom-call(f32[256,512]{1,0:T(8,128)S(1)} %get-tuple-element.15.refs_0_, bf16[256,512]{1,0:T(8,128)(2,1)S(1)} %collective-permute-done.8.refs_1_, bf16[256,512]{1,0:T(8,128)(2,1)S(1)} %collective-permute-done.9.refs_2_, bf16[256,512]{1,0:T(8,128)(2,1)S(1)} %collective-permute-done.10.refs_3_, ...), custom_call_target="tpu_custom_call" | custom-call | tf_op jit(solution)/shard_map/pallas_call | solution.py:159
  (16 shorter events, 0.0 us)
Async XLA Ops:
  0.7 1.0 %copy-start.1 = (bf16[1,1,16,128,128]{4,3,2,1,0:T(8,128)(2,1)S(1)}, bf16[1,1,16,128,128]{4,3,2,1,0:T(8,128)(2,1)}, u32[]{:S(2)}) copy-start(bf16[1,1,16,128,128]{4,3,2,1,0:T(8,128)(2,1)} %blocks_ref.1) | copy-start | bytes 1572868
  1.7 0.7 %copy-start.3 = (s32[1024]{0:T(1024)S(1)}, s32[1024]{0:T(1024)}, u32[]{:S(2)}) copy-start(s32[1024]{0:T(1024)} %param.7) | copy-start | bytes 12292
  2.4 0.7 %copy-start.4 = (s32[1,1,16]{2,1,0:T(1,128)S(1)}, s32[1,1,16]{2,1,0:T(1,128)}, u32[]{:S(2)}) copy-start(s32[1,1,16]{2,1,0:T(1,128)} %slots_ref.1) | copy-start | bytes 196
  4.3 22.4 %collective-permute-start = (bf16[1024,1024]{1,0:T(8,128)(2,1)S(1)}, bf16[1024,1024]{1,0:T(8,128)(2,1)S(1)}, u32[]{:S(2)}, u32[]{:S(2)}) collective-permute-start(bf16[1024,1024]{1,0:T(8,128)(2,1)S(1)} %get-tuple-element.14), channel_id=1, source_target_pairs={{0,1},{1,0},{2,3},{3,2},{4,5},{5,4},{6,7},{7,6},{8,9},{9,8},{10,11... | collective-permute-start | bytes 6291464 | tf_op jit(solution)/shard_map/ppermute | solution.py:114
  6.2 10.7 %collective-permute-start.1 = (bf16[256,512]{1,0:T(8,128)(2,1)}, bf16[256,512]{1,0:T(8,128)(2,1)S(1)}, u32[]{:S(2)}, u32[]{:S(2)}) collective-permute-start(bf16[256,512]{1,0:T(8,128)(2,1)} %refs_0_.1), channel_id=1, source_target_pairs={{0,8},{8,0},{16,24},{24,16},{1,9},{9,1},{17,25},{25,17},{2,10},{10... | collective-permute-start | bytes 786440 | tf_op jit(solution)/shard_map/ppermute | solution.py:133
  9.6 13.7 %collective-permute-start.2 = (bf16[256,512]{1,0:T(8,128)(2,1)}, bf16[256,512]{1,0:T(8,128)(2,1)S(1)}, u32[]{:S(2)}, u32[]{:S(2)}) collective-permute-start(bf16[256,512]{1,0:T(8,128)(2,1)} %refs_0_.1), channel_id=1, source_target_pairs={{0,16},{8,24},{16,0},{24,8},{1,17},{9,25},{17,1},{25,9},{2,18},{10... | collective-permute-start | bytes 786440 | tf_op jit(solution)/shard_map/ppermute | solution.py:133
  11.3 13.8 %collective-permute-start.3 = (bf16[256,512]{1,0:T(8,128)(2,1)}, bf16[256,512]{1,0:T(8,128)(2,1)S(1)}, u32[]{:S(2)}, u32[]{:S(2)}) collective-permute-start(bf16[256,512]{1,0:T(8,128)(2,1)} %refs_0_.1), channel_id=1, source_target_pairs={{0,24},{8,16},{16,8},{24,0},{1,25},{9,17},{17,9},{25,1},{2,26},{10... | collective-permute-start | bytes 786440 | tf_op jit(solution)/shard_map/ppermute | solution.py:133
  12.7 12.5 %collective-permute-start.4 = (bf16[256,512]{1,0:T(8,128)(2,1)}, bf16[256,512]{1,0:T(8,128)(2,1)S(1)}, u32[]{:S(2)}, u32[]{:S(2)}) collective-permute-start(bf16[256,512]{1,0:T(8,128)(2,1)} %refs_0_.1), channel_id=1, source_target_pairs={{0,1},{1,0},{2,3},{3,2},{4,5},{5,4},{6,7},{7,6},{8,9},{9,8},{10,11... | collective-permute-start | bytes 786440 | tf_op jit(solution)/shard_map/ppermute | solution.py:114
  16.9 8.3 %collective-permute-start.5 = (bf16[256,512]{1,0:T(8,128)(2,1)S(1)}, bf16[256,512]{1,0:T(8,128)(2,1)S(1)}, u32[]{:S(2)}, u32[]{:S(2)}) collective-permute-start(bf16[256,512]{1,0:T(8,128)(2,1)S(1)} %collective-permute-done.1.refs_1_), channel_id=1, source_target_pairs={{0,1},{1,0},{2,3},{3,2},{4,5},{5,4},{6,7},{7,6},{8,9},{9,8},{10,11... | collective-permute-start | bytes 786440 | tf_op jit(solution)/shard_map/ppermute | solution.py:114
  23.3 1.8 %collective-permute-start.6 = (bf16[256,512]{1,0:T(8,128)(2,1)S(1)}, bf16[256,512]{1,0:T(8,128)(2,1)S(1)}, u32[]{:S(2)}, u32[]{:S(2)}) collective-permute-start(bf16[256,512]{1,0:T(8,128)(2,1)S(1)} %collective-permute-done.2.refs_2_), channel_id=1, source_target_pairs={{0,1},{1,0},{2,3},{3,2},{4,5},{5,4},{6,7},{7,6},{8,9},{9,8},{10,11... | collective-permute-start | bytes 786440 | tf_op jit(solution)/shard_map/ppermute | solution.py:114
  25.1 1.5 %collective-permute-start.7 = (bf16[256,512]{1,0:T(8,128)(2,1)S(1)}, bf16[256,512]{1,0:T(8,128)(2,1)S(1)}, u32[]{:S(2)}, u32[]{:S(2)}) collective-permute-start(bf16[256,512]{1,0:T(8,128)(2,1)S(1)} %collective-permute-done.3.refs_3_), channel_id=1, source_target_pairs={{0,1},{1,0},{2,3},{3,2},{4,5},{5,4},{6,7},{7,6},{8,9},{9,8},{10,11... | collective-permute-start | bytes 786440 | tf_op jit(solution)/shard_map/ppermute | solution.py:114
  26.7 1.3 %copy-start.5 = (bf16[1024,1024]{1,0:T(8,128)(2,1)}, bf16[1024,1024]{1,0:T(8,128)(2,1)S(1)}, u32[]{:S(2)}) copy-start(bf16[1024,1024]{1,0:T(8,128)(2,1)S(1)} %collective-permute-done.other_tile_ref) | copy-start | bytes 6291460
  28.0 0.9 %copy-start.2 = (bf16[256,512]{1,0:T(8,128)(2,1)S(1)}, bf16[256,512]{1,0:T(8,128)(2,1)}, u32[]{:S(2)}) copy-start(bf16[256,512]{1,0:T(8,128)(2,1)} %refs_0_.1) | copy-start | bytes 786436
  29.0 29.3 %copy-start = (bf16[512,512]{1,0:T(8,128)(2,1)S(1)}, bf16[512,512]{1,0:T(8,128)(2,1)}, u32[]{:S(2)}) copy-start(bf16[512,512]{1,0:T(8,128)(2,1)} %refs_6_.1) | copy-start | bytes 1572868
  32.9 8.4 %collective-permute-start.8 = (bf16[256,512]{1,0:T(8,128)(2,1)S(1)}, bf16[256,512]{1,0:T(8,128)(2,1)S(1)}, u32[]{:S(2)}, u32[]{:S(2)}) collective-permute-start(bf16[256,512]{1,0:T(8,128)(2,1)S(1)} %get-tuple-element.16), channel_id=1, source_target_pairs={{0,2},{1,3},{2,0},{3,1},{4,6},{5,7},{6,4},{7,5},{8,10},{9,11},{10,... | collective-permute-start | bytes 786440 | tf_op jit(solution)/shard_map/ppermute | solution.py:98
  34.1 10.7 %collective-permute-start.9 = (bf16[256,512]{1,0:T(8,128)(2,1)S(1)}, bf16[256,512]{1,0:T(8,128)(2,1)S(1)}, u32[]{:S(2)}, u32[]{:S(2)}) collective-permute-start(bf16[256,512]{1,0:T(8,128)(2,1)S(1)} %get-tuple-element.19), channel_id=1, source_target_pairs={{2,4},{3,5},{4,2},{5,3},{10,12},{11,13},{12,10},{13,11},{18,20},{1... | collective-permute-start | bytes 786440 | tf_op jit(solution)/shard_map/ppermute | solution.py:98
  41.4 9.7 %collective-permute-start.10 = (bf16[256,512]{1,0:T(8,128)(2,1)S(1)}, bf16[256,512]{1,0:T(8,128)(2,1)S(1)}, u32[]{:S(2)}, u32[]{:S(2)}) collective-permute-start(bf16[256,512]{1,0:T(8,128)(2,1)S(1)} %get-tuple-element.19), channel_id=1, source_target_pairs={{0,2},{1,3},{6,4},{7,5},{8,10},{9,11},{14,12},{15,13},{16,18},{17,... | collective-permute-start | bytes 786440 | tf_op jit(solution)/shard_map/ppermute | solution.py:98
  44.4 13.8 %collective-permute-start.11 = (bf16[256,512]{1,0:T(8,128)(2,1)S(1)}, bf16[256,512]{1,0:T(8,128)(2,1)S(1)}, u32[]{:S(2)}, u32[]{:S(2)}) collective-permute-start(bf16[256,512]{1,0:T(8,128)(2,1)S(1)} %fusion), channel_id=1, source_target_pairs={{0,4},{1,5},{4,0},{5,1},{2,6},{3,7},{6,2},{7,3},{8,12},{9,13},{12,... | collective-permute-start | bytes 786440 | tf_op jit(solution)/shard_map/ppermute | solution.py:98
